TPU v7x, 512 devices: a whole 4x4x16 slice. The times are simulated.
512 devices in a mesh: row: 16 (over x, y), col: 32 (over z, core).
Axes of the slice: x: 4, y: 4, z: 16, core: 2. Of those that a mesh axis runs over, the one named last changes fastest.
Arguments:
- positions: float32 [3, 32768], P(None, ('row', 'col')), may hold values from -1 to 96, as said below
- noise: float32 [8, 3, 32768], P(None, None, ('row', 'col')), may hold values from -6 to 6
Outputs:
- basis: float32 [8, 3, 32768], P(None, None, ('row', 'col'))
- residual: float32 [8, 3, 32768], P(None, None, ('row', 'col'))
- coefficients: float32 [3, 8, 8], replicated
Inputs may be any that keep to these rules, and one draw needn't show every extreme that they name: `positions`: bead k lies within 0.77 of each coordinate of its own point of a cubic lattice of spacing 2.2 with 32 by 32 points a layer, distinct beads on distinct points.
All inputs are finite; a program needn't handle non-finite values.
Results may differ from a plain program's by a relative error of at most 0.0003.
Values sent between devices are 32-bit elements; how exact they have to be, the bound alone decides.
A program may use at most 64 MiB of HBM per device.

v0:
```python
import jax
import jax.numpy as jnp
from jax import lax
from jax.sharding import PartitionSpec as P


def pair_tensor(target_pos, source_pos):
    displace = target_pos[:, :, None] - source_pos[:, None, :]
    distance_sq = jnp.sum(displace * displace, axis=0)
    distance = jnp.sqrt(distance_sq)
    safe_distance = jnp.where(distance > 0, distance, 1.0)
    safe_sq = safe_distance * safe_distance
    far_iso = 0.75 / safe_distance * (1.0 + 2.0 / (3.0 * safe_sq))
    far_dir = 0.75 / safe_distance * (1.0 - 2.0 / safe_sq) / safe_sq
    near_iso = 1.0 - 9.0 * distance / 32.0
    near_dir = 3.0 / (32.0 * safe_distance)
    intersecting = distance < 2.0
    iso_part = jnp.where(intersecting, near_iso, far_iso)
    dir_part = jnp.where(intersecting, near_dir, far_dir)
    identity = jnp.eye(3, dtype=displace.dtype)
    return identity[:, :, None, None] * iso_part + dir_part * displace[:, None] * displace[None, :]


def local_gram(left, right):
    return jnp.einsum("kan,jan->kj", left, right, precision=lax.Precision.HIGHEST)


def combine(vectors, matrix):
    return jnp.einsum("kan,kj->jan", vectors, matrix, precision=lax.Precision.HIGHEST)


def lower_inverse(factor):
    return jax.scipy.linalg.solve_triangular(
        factor, jnp.eye(factor.shape[0], dtype=factor.dtype), lower=True
    )


def local(positions, noise):
    local_beads = positions.shape[1]
    total_count = 3.0 * local_beads * lax.axis_size("row") * lax.axis_size("col")
    target_pos = lax.all_gather(positions, "row", axis=1, tiled=True)
    source_pos = lax.all_gather(positions, "col", axis=1, tiled=True)

    def mobility(vectors):
        initial = jnp.zeros((vectors.shape[0], 3, target_pos.shape[1]), jnp.float32)
        source_piece = lax.all_gather(vectors, "col", axis=2, tiled=True)
        piece_width = source_piece.shape[2]
        block_count = 1
        while piece_width % block_count != 0 or piece_width // block_count > 256:
            block_count = block_count + 1
        block_width = piece_width // block_count

        def add_block(block_index, running):
            block_pos = lax.dynamic_slice_in_dim(
                source_pos, block_index * block_width, block_width, 1
            )
            block_vectors = lax.dynamic_slice_in_dim(
                source_piece, block_index * block_width, block_width, 2
            )
            tensor = pair_tensor(target_pos, block_pos)
            return running + jnp.einsum(
                "abts,kbs->kat", tensor, block_vectors, precision=lax.Precision.HIGHEST
            )

        partial_image = lax.fori_loop(0, block_count, add_block, initial)
        summed = lax.psum(partial_image, "row")
        return lax.dynamic_slice_in_dim(summed, lax.axis_index("row") * local_beads, local_beads, 2)

    start_matrix = lax.psum(local_gram(noise, noise), ("row", "col")) / total_count
    start_factor = jnp.linalg.cholesky(start_matrix)
    first = combine(noise, lower_inverse(start_factor).T)
    image = mobility(first)
    alpha_one = lax.psum(local_gram(first, image), ("row", "col")) / total_count
    remainder = image - combine(first, alpha_one)
    residual_matrix = lax.psum(local_gram(remainder, remainder), ("row", "col")) / total_count
    factor_one = jnp.linalg.cholesky(residual_matrix)
    basis = combine(remainder, lower_inverse(factor_one).T)
    image = mobility(basis) - combine(first, factor_one)
    alpha_two = lax.psum(local_gram(basis, image), ("row", "col")) / total_count
    residual = image - combine(basis, alpha_two)
    return (basis, residual, jnp.stack([alpha_one, factor_one, alpha_two]))


def solution(mesh):
    return jax.shard_map(
        local,
        mesh=mesh,
        in_specs=(P(None, ("row", "col")), P(None, None, ("row", "col"))),
        out_specs=(P(None, None, ("row", "col")), P(None, None, ("row", "col")), P()),
        check_vma=False,
    )
```

profile of v0, /device:TPU:1, one launch (start us, length us, event | category | flops | bytes accessed | tf_op | source)
XLA Modules:
  0.0 1041.4 jit_solution(14341036072423276544)
XLA Ops:
  7.2 38.0 %all-gather.1 = f32[32,64,3]{1,2,0:T(4,128)S(1)} all-gather(f32[1,64,3]{1,2,0:T(4,128)} %bitcast.96), channel_id=1, replica_groups=mesh['row'=16,'col'=32] {'col'}, dimensions={0}, use_global_device_ids=true | all-gather | bytes 25344 | tf_op jit(solution)/shard_map/all_gather | solution.py:42
  45.2 18.3 %all-gather = f32[16,64,3]{1,2,0:T(4,128)S(1)} all-gather(f32[1,64,3]{1,2,0:T(4,128)} %bitcast.97), channel_id=1, replica_groups=mesh['row'=16,'col'=32] {'row'}, dimensions={0}, use_global_device_ids=true | all-gather | bytes 13056 | tf_op jit(solution)/shard_map/all_gather | solution.py:41
  63.7 104.2 %psum.42 = f32[8,8]{0,1:T(8,128)S(1)} all-reduce(f32[8,8]{0,1:T(8,128)S(1)} %convolution_bitcast_fusion.5), channel_id=1, replica_groups=mesh['row'=16,'col'=32] {'row','col'}, use_global_device_ids=true, to_apply=%region_0.0 | all-reduce | flops 64 | bytes 512 | tf_op jit(solution)/shard_map/psum | solution.py:69
  171.1 44.3 %all_gather.12 = f32[8,3,2048]{0,1,2:T(4,128)} all-gather(f32[8,3,64]{0,1,2:T(4,128)S(1)} %copy.36), channel_id=1, replica_groups=mesh['row'=16,'col'=32] {'col'}, dimensions={2}, use_global_device_ids=true | all-gather | bytes 202752 | tf_op jit(solution)/shard_map/all_gather | solution.py:46
  215.4 3.3 copy.39
  218.9 120.9 %while.32 = (s32[]{:T(128)}, f32[8,3,1024]{2,0,1:T(8,128)S(1)}, f32[8,3,2048]{2,0,1:T(8,128)S(1)}, f32[3,1024]{1,0:T(4,128)S(1)}, f32[3,2048]{1,0:T(4,128)S(1)},...) while((s32[]{:T(128)}, f32[8,3,1024]{2,0,1:T(8,128)S(1)}, f32[8,3,2048]{2,0,1:T(8,128)S(1)}, ...), condition=%wide.region_5.8_spmd.clone, body=%wide.region_3.7_spmd.clone.sunk | while | flops 242270240 | bytes 19134656 | solution.py:65
  219.4 2.0 multiply_select_fusion.4
  221.4 2.1 subtract_multiply_fusion.4
  223.5 10.5 %fusion.87 = f32[8,3,1024]{2,0,1:T(8,128)S(1)} fusion(f32[3,1024,256]{2,1,0:T(8,128)} %get-tuple-element.423, f32[3,1024,256]{2,1,0:T(8,128)S(1)} %get-tuple-element.424, f32[1024,256]{1,0:T(8,128)} %get-tuple-element.425, f32[3,3]{1,0:T(4,128)S(1)} %fusion.86, f32[8,3,1024]{2,0,1:T(8,128)S(1)} %get-tuple-element.445, pred[]{:T(512)S(6)} %compare.14, ...), kind=kOutput, calls=%fused_computation.13.clone.1 | convolution fusion | flops 233619456 | bytes 7563269 | tf_op jit(solution)/shard_map/while/body/eval_jaxpr/abts,kbs->kat/dot_general | solution.py:61
  234.5 2.0 multiply_select_fusion.4
  236.5 2.1 subtract_multiply_fusion.4
  238.7 10.5 %fusion.87 = f32[8,3,1024]{2,0,1:T(8,128)S(1)} fusion(f32[3,1024,256]{2,1,0:T(8,128)} %get-tuple-element.423, f32[3,1024,256]{2,1,0:T(8,128)S(1)} %get-tuple-element.424, f32[1024,256]{1,0:T(8,128)} %get-tuple-element.425, f32[3,3]{1,0:T(4,128)S(1)} %fusion.86, f32[8,3,1024]{2,0,1:T(8,128)S(1)} %get-tuple-element.445, pred[]{:T(512)S(6)} %compare.14, ...), kind=kOutput, calls=%fused_computation.13.clone.1 | convolution fusion | flops 233619456 | bytes 7563269 | tf_op jit(solution)/shard_map/while/body/eval_jaxpr/abts,kbs->kat/dot_general | solution.py:61
  251.6 2.1 subtract_multiply_fusion.4
  253.8 10.5 %fusion.87 = f32[8,3,1024]{2,0,1:T(8,128)S(1)} fusion(f32[3,1024,256]{2,1,0:T(8,128)} %get-tuple-element.423, f32[3,1024,256]{2,1,0:T(8,128)S(1)} %get-tuple-element.424, f32[1024,256]{1,0:T(8,128)} %get-tuple-element.425, f32[3,3]{1,0:T(4,128)S(1)} %fusion.86, f32[8,3,1024]{2,0,1:T(8,128)S(1)} %get-tuple-element.445, pred[]{:T(512)S(6)} %compare.14, ...), kind=kOutput, calls=%fused_computation.13.clone.1 | convolution fusion | flops 233619456 | bytes 7563269 | tf_op jit(solution)/shard_map/while/body/eval_jaxpr/abts,kbs->kat/dot_general | solution.py:61
  266.8 2.1 subtract_multiply_fusion.4
  268.9 10.5 %fusion.87 = f32[8,3,1024]{2,0,1:T(8,128)S(1)} fusion(f32[3,1024,256]{2,1,0:T(8,128)} %get-tuple-element.423, f32[3,1024,256]{2,1,0:T(8,128)S(1)} %get-tuple-element.424, f32[1024,256]{1,0:T(8,128)} %get-tuple-element.425, f32[3,3]{1,0:T(4,128)S(1)} %fusion.86, f32[8,3,1024]{2,0,1:T(8,128)S(1)} %get-tuple-element.445, pred[]{:T(512)S(6)} %compare.14, ...), kind=kOutput, calls=%fused_computation.13.clone.1 | convolution fusion | flops 233619456 | bytes 7563269 | tf_op jit(solution)/shard_map/while/body/eval_jaxpr/abts,kbs->kat/dot_general | solution.py:61
  281.9 2.1 subtract_multiply_fusion.4
  284.0 10.5 %fusion.87 = f32[8,3,1024]{2,0,1:T(8,128)S(1)} fusion(f32[3,1024,256]{2,1,0:T(8,128)} %get-tuple-element.423, f32[3,1024,256]{2,1,0:T(8,128)S(1)} %get-tuple-element.424, f32[1024,256]{1,0:T(8,128)} %get-tuple-element.425, f32[3,3]{1,0:T(4,128)S(1)} %fusion.86, f32[8,3,1024]{2,0,1:T(8,128)S(1)} %get-tuple-element.445, pred[]{:T(512)S(6)} %compare.14, ...), kind=kOutput, calls=%fused_computation.13.clone.1 | convolution fusion | flops 233619456 | bytes 7563269 | tf_op jit(solution)/shard_map/while/body/eval_jaxpr/abts,kbs->kat/dot_general | solution.py:61
  297.0 2.1 subtract_multiply_fusion.4
  299.1 10.5 %fusion.87 = f32[8,3,1024]{2,0,1:T(8,128)S(1)} fusion(f32[3,1024,256]{2,1,0:T(8,128)} %get-tuple-element.423, f32[3,1024,256]{2,1,0:T(8,128)S(1)} %get-tuple-element.424, f32[1024,256]{1,0:T(8,128)} %get-tuple-element.425, f32[3,3]{1,0:T(4,128)S(1)} %fusion.86, f32[8,3,1024]{2,0,1:T(8,128)S(1)} %get-tuple-element.445, pred[]{:T(512)S(6)} %compare.14, ...), kind=kOutput, calls=%fused_computation.13.clone.1 | convolution fusion | flops 233619456 | bytes 7563269 | tf_op jit(solution)/shard_map/while/body/eval_jaxpr/abts,kbs->kat/dot_general | solution.py:61
  312.1 2.1 subtract_multiply_fusion.4
  314.2 10.5 %fusion.87 = f32[8,3,1024]{2,0,1:T(8,128)S(1)} fusion(f32[3,1024,256]{2,1,0:T(8,128)} %get-tuple-element.423, f32[3,1024,256]{2,1,0:T(8,128)S(1)} %get-tuple-element.424, f32[1024,256]{1,0:T(8,128)} %get-tuple-element.425, f32[3,3]{1,0:T(4,128)S(1)} %fusion.86, f32[8,3,1024]{2,0,1:T(8,128)S(1)} %get-tuple-element.445, pred[]{:T(512)S(6)} %compare.14, ...), kind=kOutput, calls=%fused_computation.13.clone.1 | convolution fusion | flops 233619456 | bytes 7563269 | tf_op jit(solution)/shard_map/while/body/eval_jaxpr/abts,kbs->kat/dot_general | solution.py:61
  327.2 2.1 subtract_multiply_fusion.4
  329.4 10.5 %fusion.87 = f32[8,3,1024]{2,0,1:T(8,128)S(1)} fusion(f32[3,1024,256]{2,1,0:T(8,128)} %get-tuple-element.423, f32[3,1024,256]{2,1,0:T(8,128)S(1)} %get-tuple-element.424, f32[1024,256]{1,0:T(8,128)} %get-tuple-element.425, f32[3,3]{1,0:T(4,128)S(1)} %fusion.86, f32[8,3,1024]{2,0,1:T(8,128)S(1)} %get-tuple-element.445, pred[]{:T(512)S(6)} %compare.14, ...), kind=kOutput, calls=%fused_computation.13.clone.1 | convolution fusion | flops 233619456 | bytes 7563269 | tf_op jit(solution)/shard_map/while/body/eval_jaxpr/abts,kbs->kat/dot_general | solution.py:61
  340.6 103.5 %all-reduce.3.cloned.1.call-done = f32[8,3,1024]{2,0,1:T(8,128)} async-done(((f32[8,3,1024]{2,0,1:T(8,128)}), f32[8,3,1024]{2,0,1:T(8,128)}) %all-reduce.3.cloned.1.call-update) | async-done | bytes 98320 | tf_op jit(solution)/shard_map/psum | solution.py:66
  444.9 104.2 %psum.44 = f32[8,8]{0,1:T(8,128)S(1)} all-reduce(f32[8,8]{0,1:T(8,128)S(1)} %convolution_bitcast_fusion.3), channel_id=1, replica_groups=mesh['row'=16,'col'=32] {'row','col'}, use_global_device_ids=true, to_apply=%region_7.10 | all-reduce | flops 64 | bytes 512 | tf_op jit(solution)/shard_map/psum | solution.py:73
  550.1 100.2 %psum.45 = f32[8,8]{0,1:T(8,128)S(1)} all-reduce(f32[8,8]{0,1:T(8,128)S(1)} %convolution_bitcast_fusion.2), channel_id=1, replica_groups=mesh['row'=16,'col'=32] {'row','col'}, use_global_device_ids=true, to_apply=%region_8.11 | all-reduce | flops 64 | bytes 512 | tf_op jit(solution)/shard_map/psum | solution.py:75
  653.5 43.3 %all_gather.15 = f32[8,3,2048]{0,1,2:T(4,128)} all-gather(f32[8,3,64]{0,1,2:T(4,128)S(1)} %copy.44), channel_id=1, replica_groups=mesh['row'=16,'col'=32] {'col'}, dimensions={2}, use_global_device_ids=true | all-gather | bytes 202752 | tf_op jit(solution)/shard_map/all_gather | solution.py:46
  696.8 3.3 copy.45
  700.1 120.9 %while.33 = (s32[]{:T(128)}, f32[8,3,1024]{2,0,1:T(8,128)S(1)}, f32[8,3,2048]{2,0,1:T(8,128)S(1)}, f32[3,1024]{1,0:T(4,128)S(1)}, f32[3,2048]{1,0:T(4,128)S(1)},...) while((s32[]{:T(128)}, f32[8,3,1024]{2,0,1:T(8,128)S(1)}, f32[8,3,2048]{2,0,1:T(8,128)S(1)}, ...), condition=%wide.region_11.14_spmd.clone, body=%wide.region_9.13_spmd.clone.sunk | while | flops 242270240 | bytes 19134656 | solution.py:65
  702.6 2.1 subtract_multiply_fusion.5
  704.8 10.5 %fusion.91 = f32[8,3,1024]{2,0,1:T(8,128)S(1)} fusion(f32[3,1024,256]{2,1,0:T(8,128)} %get-tuple-element.432, f32[3,1024,256]{2,1,0:T(8,128)S(1)} %get-tuple-element.433, f32[1024,256]{1,0:T(8,128)} %get-tuple-element.434, f32[3,3]{1,0:T(4,128)S(1)} %fusion.90, f32[8,3,1024]{2,0,1:T(8,128)S(1)} %get-tuple-element.472, pred[]{:T(512)S(6)} %compare.15, ...), kind=kOutput, calls=%fused_computation.37.clone.1 | convolution fusion | flops 233619456 | bytes 7563269 | tf_op jit(solution)/shard_map/while/body/eval_jaxpr/abts,kbs->kat/dot_general | solution.py:61
  717.8 2.1 subtract_multiply_fusion.5
  719.9 10.5 %fusion.91 = f32[8,3,1024]{2,0,1:T(8,128)S(1)} fusion(f32[3,1024,256]{2,1,0:T(8,128)} %get-tuple-element.432, f32[3,1024,256]{2,1,0:T(8,128)S(1)} %get-tuple-element.433, f32[1024,256]{1,0:T(8,128)} %get-tuple-element.434, f32[3,3]{1,0:T(4,128)S(1)} %fusion.90, f32[8,3,1024]{2,0,1:T(8,128)S(1)} %get-tuple-element.472, pred[]{:T(512)S(6)} %compare.15, ...), kind=kOutput, calls=%fused_computation.37.clone.1 | convolution fusion | flops 233619456 | bytes 7563269 | tf_op jit(solution)/shard_map/while/body/eval_jaxpr/abts,kbs->kat/dot_general | solution.py:61
  732.9 2.1 subtract_multiply_fusion.5
  735.0 10.5 %fusion.91 = f32[8,3,1024]{2,0,1:T(8,128)S(1)} fusion(f32[3,1024,256]{2,1,0:T(8,128)} %get-tuple-element.432, f32[3,1024,256]{2,1,0:T(8,128)S(1)} %get-tuple-element.433, f32[1024,256]{1,0:T(8,128)} %get-tuple-element.434, f32[3,3]{1,0:T(4,128)S(1)} %fusion.90, f32[8,3,1024]{2,0,1:T(8,128)S(1)} %get-tuple-element.472, pred[]{:T(512)S(6)} %compare.15, ...), kind=kOutput, calls=%fused_computation.37.clone.1 | convolution fusion | flops 233619456 | bytes 7563269 | tf_op jit(solution)/shard_map/while/body/eval_jaxpr/abts,kbs->kat/dot_general | solution.py:61
  748.0 2.1 subtract_multiply_fusion.5
  750.1 10.5 %fusion.91 = f32[8,3,1024]{2,0,1:T(8,128)S(1)} fusion(f32[3,1024,256]{2,1,0:T(8,128)} %get-tuple-element.432, f32[3,1024,256]{2,1,0:T(8,128)S(1)} %get-tuple-element.433, f32[1024,256]{1,0:T(8,128)} %get-tuple-element.434, f32[3,3]{1,0:T(4,128)S(1)} %fusion.90, f32[8,3,1024]{2,0,1:T(8,128)S(1)} %get-tuple-element.472, pred[]{:T(512)S(6)} %compare.15, ...), kind=kOutput, calls=%fused_computation.37.clone.1 | convolution fusion | flops 233619456 | bytes 7563269 | tf_op jit(solution)/shard_map/while/body/eval_jaxpr/abts,kbs->kat/dot_general | solution.py:61
  763.1 2.1 subtract_multiply_fusion.5
  765.2 10.5 %fusion.91 = f32[8,3,1024]{2,0,1:T(8,128)S(1)} fusion(f32[3,1024,256]{2,1,0:T(8,128)} %get-tuple-element.432, f32[3,1024,256]{2,1,0:T(8,128)S(1)} %get-tuple-element.433, f32[1024,256]{1,0:T(8,128)} %get-tuple-element.434, f32[3,3]{1,0:T(4,128)S(1)} %fusion.90, f32[8,3,1024]{2,0,1:T(8,128)S(1)} %get-tuple-element.472, pred[]{:T(512)S(6)} %compare.15, ...), kind=kOutput, calls=%fused_computation.37.clone.1 | convolution fusion | flops 233619456 | bytes 7563269 | tf_op jit(solution)/shard_map/while/body/eval_jaxpr/abts,kbs->kat/dot_general | solution.py:61
  778.2 2.1 subtract_multiply_fusion.5
  780.4 10.5 %fusion.91 = f32[8,3,1024]{2,0,1:T(8,128)S(1)} fusion(f32[3,1024,256]{2,1,0:T(8,128)} %get-tuple-element.432, f32[3,1024,256]{2,1,0:T(8,128)S(1)} %get-tuple-element.433, f32[1024,256]{1,0:T(8,128)} %get-tuple-element.434, f32[3,3]{1,0:T(4,128)S(1)} %fusion.90, f32[8,3,1024]{2,0,1:T(8,128)S(1)} %get-tuple-element.472, pred[]{:T(512)S(6)} %compare.15, ...), kind=kOutput, calls=%fused_computation.37.clone.1 | convolution fusion | flops 233619456 | bytes 7563269 | tf_op jit(solution)/shard_map/while/body/eval_jaxpr/abts,kbs->kat/dot_general | solution.py:61
  793.3 2.1 subtract_multiply_fusion.5
  795.5 10.5 %fusion.91 = f32[8,3,1024]{2,0,1:T(8,128)S(1)} fusion(f32[3,1024,256]{2,1,0:T(8,128)} %get-tuple-element.432, f32[3,1024,256]{2,1,0:T(8,128)S(1)} %get-tuple-element.433, f32[1024,256]{1,0:T(8,128)} %get-tuple-element.434, f32[3,3]{1,0:T(4,128)S(1)} %fusion.90, f32[8,3,1024]{2,0,1:T(8,128)S(1)} %get-tuple-element.472, pred[]{:T(512)S(6)} %compare.15, ...), kind=kOutput, calls=%fused_computation.37.clone.1 | convolution fusion | flops 233619456 | bytes 7563269 | tf_op jit(solution)/shard_map/while/body/eval_jaxpr/abts,kbs->kat/dot_general | solution.py:61
  808.4 2.1 subtract_multiply_fusion.5
  810.6 10.5 %fusion.91 = f32[8,3,1024]{2,0,1:T(8,128)S(1)} fusion(f32[3,1024,256]{2,1,0:T(8,128)} %get-tuple-element.432, f32[3,1024,256]{2,1,0:T(8,128)S(1)} %get-tuple-element.433, f32[1024,256]{1,0:T(8,128)} %get-tuple-element.434, f32[3,3]{1,0:T(4,128)S(1)} %fusion.90, f32[8,3,1024]{2,0,1:T(8,128)S(1)} %get-tuple-element.472, pred[]{:T(512)S(6)} %compare.15, ...), kind=kOutput, calls=%fused_computation.37.clone.1 | convolution fusion | flops 233619456 | bytes 7563269 | tf_op jit(solution)/shard_map/while/body/eval_jaxpr/abts,kbs->kat/dot_general | solution.py:61
  821.8 105.6 %all-reduce.5.cloned.1.call-done = f32[8,3,1024]{2,0,1:T(8,128)} async-done(((f32[8,3,1024]{2,0,1:T(8,128)}), f32[8,3,1024]{2,0,1:T(8,128)}) %all-reduce.5.cloned.1.call-update) | async-done | bytes 98320 | tf_op jit(solution)/shard_map/psum | solution.py:66
  929.1 104.0 %psum.47 = f32[8,8]{0,1:T(8,128)S(1)} all-reduce(f32[8,8]{0,1:T(8,128)S(1)} %convolution_bitcast_fusion), channel_id=1, replica_groups=mesh['row'=16,'col'=32] {'row','col'}, use_global_device_ids=true, to_apply=%region_13.16 | all-reduce | flops 64 | bytes 512 | tf_op jit(solution)/shard_map/psum | solution.py:79
  (114 shorter events, 49.1 us)
Async XLA Ops:
  7.2 56.4 %copy-start = (f32[8,3,64]{2,0,1:T(8,128)S(1)}, f32[8,3,64]{2,0,1:T(8,128)}, u32[]{:S(2)}) copy-start(f32[8,3,64]{2,0,1:T(8,128)} %param.10) | copy-start | bytes 18436
  7.2 436.9 %all-reduce.3.cloned.1.call-start = ((), (), s32[]{:S(2)}) async-start(), calls=%async_computation | async-start | bytes 196608 | tf_op jit(solution)/shard_map/psum | solution.py:66
  339.8 0.6 copy-start.3
  340.5 586.9 %all-reduce.5.cloned.1.call-start = ((), (), s32[]{:S(2)}) async-start(), calls=%async_computation.1 | async-start | bytes 196608 | tf_op jit(solution)/shard_map/psum | solution.py:66
  653.4 379.7 %copy-start.1 = (f32[8,3,64]{2,0,1:T(8,128)}, f32[8,3,64]{2,0,1:T(8,128)S(1)}, u32[]{:S(2)}) copy-start(f32[8,3,64]{2,0,1:T(8,128)S(1)} %fusion.61) | copy-start | bytes 18436
  821.0 0.6 copy-start.2
Sparse Core Ops, SparseCore 0:
  340.6 103.3 all-reduce.2
  821.8 105.5 all-reduce.4
where the time goes:
time: 1040 us
  blocking collectives  556 us (53%)
  waiting for transfers between devices  209 us (20%)
  matrix products  173 us (17%)
  other arithmetic  80.1 us (8%)
  between operations  14.1 us (1%)
    psum x2, waiting for transfers between devices, mobility(): summed = lax.psum(partial_image, 'row')  209 us
    dot_general x16, matrix products, add_block(): jnp.einsum('abts,kbs->kat', tensor, block_vectors, precision=lax.Precisio...  168 us
    psum x1, blocking collectives, local(): lax.psum(local_gram(noise, noise), ('row', 'col')) / total_count  104 us
    psum x1, blocking collectives, local(): alpha_one = lax.psum(local_gram(first, image), ('row', 'col')) / total_count  104 us
    psum x1, blocking collectives, local(): alpha_two = lax.psum(local_gram(basis, image), ('row', 'col')) / total_count  104 us
    psum x1, blocking collectives, local(): lax.psum(local_gram(remainder, remainder), ('row', 'col')) / total_count  100 us
    all_gather x2, blocking collectives, mobility(): source_piece = lax.all_gather(vectors, 'col', axis=2, tiled=True)  87.6 us
    all_gather x1, blocking collectives, local(): source_pos = lax.all_gather(positions, 'col', axis=1, tiled=True)  38 us
  transfers between devices with their start and end apart: 2, of which 2 were waited for; matrix products, arithmetic and copies ran while one was open for 0% of the time, Pallas kernels for 0%

commit v1 on v0

--- a/solution.py
+++ b/solution.py
@@ -43,7 +43,8 @@
 
     def mobility(vectors):
         initial = jnp.zeros((vectors.shape[0], 3, target_pos.shape[1]), jnp.float32)
-        source_piece = lax.all_gather(vectors, "col", axis=2, tiled=True)
+        sent = jnp.stack([vectors] * lax.axis_size("col"))
+        source_piece = jnp.concatenate(lax.all_to_all(sent, "col", 0, 0), axis=2)
         piece_width = source_piece.shape[2]
         block_count = 1
         while piece_width % block_count != 0 or piece_width // block_count > 256:

time: 1040 us -> 998 us (0.960)
  blocking collectives: 556 us -> 471 us
  waiting for transfers between devices: 209 us -> 234 us
  starting transfers between devices: 0.08 us -> 17.1 us
    all_gather x2 -> x0, blocking collectives: 87.6 us -> none  [mobility(): source_piece = lax.all_gather(vectors, 'col', axis=2, tiled=True)]
    all_to_all x0 -> x2, waiting for transfers between devices: none -> 18.7 us  [mobility(): source_piece = jnp.concatenate(lax.all_to_all(sent, 'col', 0, 0), axis=2)]
    all_to_all x0 -> x2, starting transfers between devices: none -> 17 us  [mobility(): source_piece = jnp.concatenate(lax.all_to_all(sent, 'col', 0, 0), axis=2)]
  transfers between devices with their start and end apart: 2 -> 4, of which waited for: 2 -> 3; matrix products, arithmetic and copies ran while one was open for 0% -> 0% of each run, Pallas kernels for 0% -> 0%
where the time goes in v1:
time: 998 us; the launch traced here: 997 us
  blocking collectives  471 us (47%)
  waiting for transfers between devices  234 us (23%)
  matrix products  173 us (17%)
  other arithmetic  82.3 us (8%)
  starting transfers between devices  17.1 us (2%)
  between operations  14.2 us (1%)
    psum x2, waiting for transfers between devices, mobility(): summed = lax.psum(partial_image, 'row')  215 us
    dot_general x16, matrix products, add_block(): jnp.einsum('abts,kbs->kat', tensor, block_vectors, precision=lax.Precisio...  168 us
    psum x1, blocking collectives, local(): lax.psum(local_gram(noise, noise), ('row', 'col')) / total_count  111 us
    psum x1, blocking collectives, local(): alpha_one = lax.psum(local_gram(first, image), ('row', 'col')) / total_count  104 us
    psum x1, blocking collectives, local(): alpha_two = lax.psum(local_gram(basis, image), ('row', 'col')) / total_count  104 us
    psum x1, blocking collectives, local(): lax.psum(local_gram(remainder, remainder), ('row', 'col')) / total_count  100 us
    all_gather x1, blocking collectives, local(): source_pos = lax.all_gather(positions, 'col', axis=1, tiled=True)  35.8 us
    mul x16, other arithmetic, pair_tensor(): dir_part * displace[:, None] * displace[None, :]  34.2 us
  transfers between devices with their start and end apart: 4, of which 3 were waited for; matrix products, arithmetic and copies ran while one was open for 0% of the time, Pallas kernels for 0%

profile of v1, /device:TPU:1, one launch (start us, length us, event | category | flops | bytes accessed | tf_op | source)
XLA Modules:
  0.0 996.6 jit_solution(16425164572195571710)
XLA Ops:
  8.0 111.0 %psum.42 = f32[8,8]{0,1:T(8,128)S(1)} all-reduce(f32[8,8]{0,1:T(8,128)S(1)} %convolution_bitcast_fusion.5), channel_id=1, replica_groups=mesh['row'=16,'col'=32] {'row','col'}, use_global_device_ids=true, to_apply=%region_0.0 | all-reduce | flops 64 | bytes 512 | tf_op jit(solution)/shard_map/psum | solution.py:70
  123.1 8.4 all-to-all-start
  131.5 35.8 %all-gather.1 = f32[32,64,3]{1,2,0:T(4,128)S(1)} all-gather(f32[1,64,3]{1,2,0:T(4,128)} %bitcast.116), channel_id=1, replica_groups=mesh['row'=16,'col'=32] {'col'}, dimensions={0}, use_global_device_ids=true | all-gather | bytes 25344 | tf_op jit(solution)/shard_map/all_gather | solution.py:42
  167.3 16.0 %all-gather = f32[16,64,3]{1,2,0:T(4,128)S(1)} all-gather(f32[1,64,3]{1,2,0:T(4,128)} %bitcast.117), channel_id=1, replica_groups=mesh['row'=16,'col'=32] {'row'}, dimensions={0}, use_global_device_ids=true | all-gather | bytes 13056 | tf_op jit(solution)/shard_map/all_gather | solution.py:41
  185.4 120.9 %while.32 = (s32[]{:T(128)}, f32[8,3,1024]{2,0,1:T(8,128)S(1)}, f32[8,3,2048]{2,0,1:T(8,128)S(1)}, f32[3,1024]{1,0:T(4,128)S(1)}, f32[3,2048]{1,0:T(4,128)S(1)},...) while((s32[]{:T(128)}, f32[8,3,1024]{2,0,1:T(8,128)S(1)}, f32[8,3,2048]{2,0,1:T(8,128)S(1)}, ...), condition=%wide.region_5.8_spmd.clone, body=%wide.region_3.7_spmd.clone.sunk | while | flops 242270240 | bytes 19134656 | solution.py:66
  185.9 2.0 multiply_select_fusion.4
  187.9 2.1 subtract_multiply_fusion.4
  190.1 10.5 %fusion.87 = f32[8,3,1024]{2,0,1:T(8,128)S(1)} fusion(f32[3,1024,256]{2,1,0:T(8,128)} %get-tuple-element.403, f32[3,1024,256]{2,1,0:T(8,128)S(1)} %get-tuple-element.404, f32[1024,256]{1,0:T(8,128)} %get-tuple-element.405, f32[3,3]{1,0:T(4,128)S(1)} %fusion.86, f32[8,3,1024]{2,0,1:T(8,128)S(1)} %get-tuple-element.425, pred[]{:T(512)S(6)} %compare.14, ...), kind=kOutput, calls=%fused_computation.13.clone.1 | convolution fusion | flops 233619456 | bytes 7563269 | tf_op jit(solution)/shard_map/while/body/eval_jaxpr/abts,kbs->kat/dot_general | solution.py:62
  201.0 2.0 multiply_select_fusion.4
  203.0 2.1 subtract_multiply_fusion.4
  205.2 10.5 %fusion.87 = f32[8,3,1024]{2,0,1:T(8,128)S(1)} fusion(f32[3,1024,256]{2,1,0:T(8,128)} %get-tuple-element.403, f32[3,1024,256]{2,1,0:T(8,128)S(1)} %get-tuple-element.404, f32[1024,256]{1,0:T(8,128)} %get-tuple-element.405, f32[3,3]{1,0:T(4,128)S(1)} %fusion.86, f32[8,3,1024]{2,0,1:T(8,128)S(1)} %get-tuple-element.425, pred[]{:T(512)S(6)} %compare.14, ...), kind=kOutput, calls=%fused_computation.13.clone.1 | convolution fusion | flops 233619456 | bytes 7563269 | tf_op jit(solution)/shard_map/while/body/eval_jaxpr/abts,kbs->kat/dot_general | solution.py:62
  216.2 2.0 multiply_select_fusion.4
  218.2 2.1 subtract_multiply_fusion.4
  220.3 10.5 %fusion.87 = f32[8,3,1024]{2,0,1:T(8,128)S(1)} fusion(f32[3,1024,256]{2,1,0:T(8,128)} %get-tuple-element.403, f32[3,1024,256]{2,1,0:T(8,128)S(1)} %get-tuple-element.404, f32[1024,256]{1,0:T(8,128)} %get-tuple-element.405, f32[3,3]{1,0:T(4,128)S(1)} %fusion.86, f32[8,3,1024]{2,0,1:T(8,128)S(1)} %get-tuple-element.425, pred[]{:T(512)S(6)} %compare.14, ...), kind=kOutput, calls=%fused_computation.13.clone.1 | convolution fusion | flops 233619456 | bytes 7563269 | tf_op jit(solution)/shard_map/while/body/eval_jaxpr/abts,kbs->kat/dot_general | solution.py:62
  233.3 2.1 subtract_multiply_fusion.4
  235.4 10.5 %fusion.87 = f32[8,3,1024]{2,0,1:T(8,128)S(1)} fusion(f32[3,1024,256]{2,1,0:T(8,128)} %get-tuple-element.403, f32[3,1024,256]{2,1,0:T(8,128)S(1)} %get-tuple-element.404, f32[1024,256]{1,0:T(8,128)} %get-tuple-element.405, f32[3,3]{1,0:T(4,128)S(1)} %fusion.86, f32[8,3,1024]{2,0,1:T(8,128)S(1)} %get-tuple-element.425, pred[]{:T(512)S(6)} %compare.14, ...), kind=kOutput, calls=%fused_computation.13.clone.1 | convolution fusion | flops 233619456 | bytes 7563269 | tf_op jit(solution)/shard_map/while/body/eval_jaxpr/abts,kbs->kat/dot_general | solution.py:62
  248.4 2.1 subtract_multiply_fusion.4
  250.5 10.5 %fusion.87 = f32[8,3,1024]{2,0,1:T(8,128)S(1)} fusion(f32[3,1024,256]{2,1,0:T(8,128)} %get-tuple-element.403, f32[3,1024,256]{2,1,0:T(8,128)S(1)} %get-tuple-element.404, f32[1024,256]{1,0:T(8,128)} %get-tuple-element.405, f32[3,3]{1,0:T(4,128)S(1)} %fusion.86, f32[8,3,1024]{2,0,1:T(8,128)S(1)} %get-tuple-element.425, pred[]{:T(512)S(6)} %compare.14, ...), kind=kOutput, calls=%fused_computation.13.clone.1 | convolution fusion | flops 233619456 | bytes 7563269 | tf_op jit(solution)/shard_map/while/body/eval_jaxpr/abts,kbs->kat/dot_general | solution.py:62
  263.5 2.1 subtract_multiply_fusion.4
  265.7 10.5 %fusion.87 = f32[8,3,1024]{2,0,1:T(8,128)S(1)} fusion(f32[3,1024,256]{2,1,0:T(8,128)} %get-tuple-element.403, f32[3,1024,256]{2,1,0:T(8,128)S(1)} %get-tuple-element.404, f32[1024,256]{1,0:T(8,128)} %get-tuple-element.405, f32[3,3]{1,0:T(4,128)S(1)} %fusion.86, f32[8,3,1024]{2,0,1:T(8,128)S(1)} %get-tuple-element.425, pred[]{:T(512)S(6)} %compare.14, ...), kind=kOutput, calls=%fused_computation.13.clone.1 | convolution fusion | flops 233619456 | bytes 7563269 | tf_op jit(solution)/shard_map/while/body/eval_jaxpr/abts,kbs->kat/dot_general | solution.py:62
  278.6 2.1 subtract_multiply_fusion.4
  280.8 10.5 %fusion.87 = f32[8,3,1024]{2,0,1:T(8,128)S(1)} fusion(f32[3,1024,256]{2,1,0:T(8,128)} %get-tuple-element.403, f32[3,1024,256]{2,1,0:T(8,128)S(1)} %get-tuple-element.404, f32[1024,256]{1,0:T(8,128)} %get-tuple-element.405, f32[3,3]{1,0:T(4,128)S(1)} %fusion.86, f32[8,3,1024]{2,0,1:T(8,128)S(1)} %get-tuple-element.425, pred[]{:T(512)S(6)} %compare.14, ...), kind=kOutput, calls=%fused_computation.13.clone.1 | convolution fusion | flops 233619456 | bytes 7563269 | tf_op jit(solution)/shard_map/while/body/eval_jaxpr/abts,kbs->kat/dot_general | solution.py:62
  293.7 2.1 subtract_multiply_fusion.4
  295.9 10.5 %fusion.87 = f32[8,3,1024]{2,0,1:T(8,128)S(1)} fusion(f32[3,1024,256]{2,1,0:T(8,128)} %get-tuple-element.403, f32[3,1024,256]{2,1,0:T(8,128)S(1)} %get-tuple-element.404, f32[1024,256]{1,0:T(8,128)} %get-tuple-element.405, f32[3,3]{1,0:T(4,128)S(1)} %fusion.86, f32[8,3,1024]{2,0,1:T(8,128)S(1)} %get-tuple-element.425, pred[]{:T(512)S(6)} %compare.14, ...), kind=kOutput, calls=%fused_computation.13.clone.1 | convolution fusion | flops 233619456 | bytes 7563269 | tf_op jit(solution)/shard_map/while/body/eval_jaxpr/abts,kbs->kat/dot_general | solution.py:62
  307.0 114.0 %all-reduce.3.cloned.1.call-done = f32[8,3,1024]{2,0,1:T(8,128)} async-done(((f32[8,3,1024]{2,0,1:T(8,128)}), f32[8,3,1024]{2,0,1:T(8,128)}) %all-reduce.3.cloned.1.call-update) | async-done | bytes 98320 | tf_op jit(solution)/shard_map/psum | solution.py:67
  421.9 104.0 %psum.44 = f32[8,8]{0,1:T(8,128)S(1)} all-reduce(f32[8,8]{0,1:T(8,128)S(1)} %convolution_bitcast_fusion.3), channel_id=1, replica_groups=mesh['row'=16,'col'=32] {'row','col'}, use_global_device_ids=true, to_apply=%region_7.10 | all-reduce | flops 64 | bytes 512 | tf_op jit(solution)/shard_map/psum | solution.py:74
  526.9 100.2 %psum.45 = f32[8,8]{0,1:T(8,128)S(1)} all-reduce(f32[8,8]{0,1:T(8,128)S(1)} %convolution_bitcast_fusion.2), channel_id=1, replica_groups=mesh['row'=16,'col'=32] {'row','col'}, use_global_device_ids=true, to_apply=%region_8.11 | all-reduce | flops 64 | bytes 512 | tf_op jit(solution)/shard_map/psum | solution.py:76
  631.1 8.7 all-to-all-start.1
  639.9 18.7 %all-to-all-done.1 = f32[32,1,1536]{2,1,0:T(1,128)S(1)} async-done(((f32[32,1,1536]{2,1,0:T(1,128)}), f32[32,1,1536]{2,1,0:T(1,128)S(1)}, u32[]{:S(2)}, u32[]{:S(2)}) %all-to-all-start.1) | async-done | bytes 196640 | tf_op jit(solution)/shard_map/all_to_all | solution.py:47
  660.1 120.9 %while.33 = (s32[]{:T(128)}, f32[8,3,1024]{2,0,1:T(8,128)S(1)}, f32[8,3,2048]{2,0,1:T(8,128)S(1)}, f32[3,1024]{1,0:T(4,128)S(1)}, f32[3,2048]{1,0:T(4,128)S(1)},...) while((s32[]{:T(128)}, f32[8,3,1024]{2,0,1:T(8,128)S(1)}, f32[8,3,2048]{2,0,1:T(8,128)S(1)}, ...), condition=%wide.region_11.14_spmd.clone, body=%wide.region_9.13_spmd.clone.sunk | while | flops 242270240 | bytes 19134656 | solution.py:66
  662.6 2.1 subtract_multiply_fusion.5
  664.8 10.5 %fusion.91 = f32[8,3,1024]{2,0,1:T(8,128)S(1)} fusion(f32[3,1024,256]{2,1,0:T(8,128)} %get-tuple-element.412, f32[3,1024,256]{2,1,0:T(8,128)S(1)} %get-tuple-element.413, f32[1024,256]{1,0:T(8,128)} %get-tuple-element.414, f32[3,3]{1,0:T(4,128)S(1)} %fusion.90, f32[8,3,1024]{2,0,1:T(8,128)S(1)} %get-tuple-element.452, pred[]{:T(512)S(6)} %compare.15, ...), kind=kOutput, calls=%fused_computation.37.clone.1 | convolution fusion | flops 233619456 | bytes 7563269 | tf_op jit(solution)/shard_map/while/body/eval_jaxpr/abts,kbs->kat/dot_general | solution.py:62
  677.7 2.1 subtract_multiply_fusion.5
  679.9 10.5 %fusion.91 = f32[8,3,1024]{2,0,1:T(8,128)S(1)} fusion(f32[3,1024,256]{2,1,0:T(8,128)} %get-tuple-element.412, f32[3,1024,256]{2,1,0:T(8,128)S(1)} %get-tuple-element.413, f32[1024,256]{1,0:T(8,128)} %get-tuple-element.414, f32[3,3]{1,0:T(4,128)S(1)} %fusion.90, f32[8,3,1024]{2,0,1:T(8,128)S(1)} %get-tuple-element.452, pred[]{:T(512)S(6)} %compare.15, ...), kind=kOutput, calls=%fused_computation.37.clone.1 | convolution fusion | flops 233619456 | bytes 7563269 | tf_op jit(solution)/shard_map/while/body/eval_jaxpr/abts,kbs->kat/dot_general | solution.py:62
  692.9 2.1 subtract_multiply_fusion.5
  695.0 10.5 %fusion.91 = f32[8,3,1024]{2,0,1:T(8,128)S(1)} fusion(f32[3,1024,256]{2,1,0:T(8,128)} %get-tuple-element.412, f32[3,1024,256]{2,1,0:T(8,128)S(1)} %get-tuple-element.413, f32[1024,256]{1,0:T(8,128)} %get-tuple-element.414, f32[3,3]{1,0:T(4,128)S(1)} %fusion.90, f32[8,3,1024]{2,0,1:T(8,128)S(1)} %get-tuple-element.452, pred[]{:T(512)S(6)} %compare.15, ...), kind=kOutput, calls=%fused_computation.37.clone.1 | convolution fusion | flops 233619456 | bytes 7563269 | tf_op jit(solution)/shard_map/while/body/eval_jaxpr/abts,kbs->kat/dot_general | solution.py:62
  708.0 2.1 subtract_multiply_fusion.5
  710.1 10.5 %fusion.91 = f32[8,3,1024]{2,0,1:T(8,128)S(1)} fusion(f32[3,1024,256]{2,1,0:T(8,128)} %get-tuple-element.412, f32[3,1024,256]{2,1,0:T(8,128)S(1)} %get-tuple-element.413, f32[1024,256]{1,0:T(8,128)} %get-tuple-element.414, f32[3,3]{1,0:T(4,128)S(1)} %fusion.90, f32[8,3,1024]{2,0,1:T(8,128)S(1)} %get-tuple-element.452, pred[]{:T(512)S(6)} %compare.15, ...), kind=kOutput, calls=%fused_computation.37.clone.1 | convolution fusion | flops 233619456 | bytes 7563269 | tf_op jit(solution)/shard_map/while/body/eval_jaxpr/abts,kbs->kat/dot_general | solution.py:62
  723.1 2.1 subtract_multiply_fusion.5
  725.2 10.5 %fusion.91 = f32[8,3,1024]{2,0,1:T(8,128)S(1)} fusion(f32[3,1024,256]{2,1,0:T(8,128)} %get-tuple-element.412, f32[3,1024,256]{2,1,0:T(8,128)S(1)} %get-tuple-element.413, f32[1024,256]{1,0:T(8,128)} %get-tuple-element.414, f32[3,3]{1,0:T(4,128)S(1)} %fusion.90, f32[8,3,1024]{2,0,1:T(8,128)S(1)} %get-tuple-element.452, pred[]{:T(512)S(6)} %compare.15, ...), kind=kOutput, calls=%fused_computation.37.clone.1 | convolution fusion | flops 233619456 | bytes 7563269 | tf_op jit(solution)/shard_map/while/body/eval_jaxpr/abts,kbs->kat/dot_general | solution.py:62
  738.2 2.1 subtract_multiply_fusion.5
  740.3 10.5 %fusion.91 = f32[8,3,1024]{2,0,1:T(8,128)S(1)} fusion(f32[3,1024,256]{2,1,0:T(8,128)} %get-tuple-element.412, f32[3,1024,256]{2,1,0:T(8,128)S(1)} %get-tuple-element.413, f32[1024,256]{1,0:T(8,128)} %get-tuple-element.414, f32[3,3]{1,0:T(4,128)S(1)} %fusion.90, f32[8,3,1024]{2,0,1:T(8,128)S(1)} %get-tuple-element.452, pred[]{:T(512)S(6)} %compare.15, ...), kind=kOutput, calls=%fused_computation.37.clone.1 | convolution fusion | flops 233619456 | bytes 7563269 | tf_op jit(solution)/shard_map/while/body/eval_jaxpr/abts,kbs->kat/dot_general | solution.py:62
  753.3 2.1 subtract_multiply_fusion.5
  755.5 10.5 %fusion.91 = f32[8,3,1024]{2,0,1:T(8,128)S(1)} fusion(f32[3,1024,256]{2,1,0:T(8,128)} %get-tuple-element.412, f32[3,1024,256]{2,1,0:T(8,128)S(1)} %get-tuple-element.413, f32[1024,256]{1,0:T(8,128)} %get-tuple-element.414, f32[3,3]{1,0:T(4,128)S(1)} %fusion.90, f32[8,3,1024]{2,0,1:T(8,128)S(1)} %get-tuple-element.452, pred[]{:T(512)S(6)} %compare.15, ...), kind=kOutput, calls=%fused_computation.37.clone.1 | convolution fusion | flops 233619456 | bytes 7563269 | tf_op jit(solution)/shard_map/while/body/eval_jaxpr/abts,kbs->kat/dot_general | solution.py:62
  768.4 2.1 subtract_multiply_fusion.5
  770.6 10.5 %fusion.91 = f32[8,3,1024]{2,0,1:T(8,128)S(1)} fusion(f32[3,1024,256]{2,1,0:T(8,128)} %get-tuple-element.412, f32[3,1024,256]{2,1,0:T(8,128)S(1)} %get-tuple-element.413, f32[1024,256]{1,0:T(8,128)} %get-tuple-element.414, f32[3,3]{1,0:T(4,128)S(1)} %fusion.90, f32[8,3,1024]{2,0,1:T(8,128)S(1)} %get-tuple-element.452, pred[]{:T(512)S(6)} %compare.15, ...), kind=kOutput, calls=%fused_computation.37.clone.1 | convolution fusion | flops 233619456 | bytes 7563269 | tf_op jit(solution)/shard_map/while/body/eval_jaxpr/abts,kbs->kat/dot_general | solution.py:62
  781.8 100.8 %all-reduce.5.cloned.1.call-done = f32[8,3,1024]{2,0,1:T(8,128)} async-done(((f32[8,3,1024]{2,0,1:T(8,128)}), f32[8,3,1024]{2,0,1:T(8,128)}) %all-reduce.5.cloned.1.call-update) | async-done | bytes 98320 | tf_op jit(solution)/shard_map/psum | solution.py:67
  884.3 104.0 %psum.47 = f32[8,8]{0,1:T(8,128)S(1)} all-reduce(f32[8,8]{0,1:T(8,128)S(1)} %convolution_bitcast_fusion), channel_id=1, replica_groups=mesh['row'=16,'col'=32] {'row','col'}, use_global_device_ids=true, to_apply=%region_13.16 | all-reduce | flops 64 | bytes 512 | tf_op jit(solution)/shard_map/psum | solution.py:80
  (127 shorter events, 52.9 us)
Async XLA Ops:
  7.2 0.7 copy-start
  123.1 60.3 %all-to-all-start = ((f32[32,1,1536]{2,1,0:T(1,128)}), f32[32,1,1536]{2,1,0:T(1,128)S(1)}, u32[]{:S(2)}, u32[]{:S(2)}) async-start(f32[32,1,1536]{2,1,0:T(1,128)} %reshape.149), calls=%async_computation | async-start | bytes 393216 | tf_op jit(solution)/shard_map/all_to_all | solution.py:47
  131.4 289.6 %all-reduce.3.cloned.1.call-start = ((), (), s32[]{:S(2)}) async-start(), calls=%async_computation.2 | async-start | bytes 196608 | tf_op jit(solution)/shard_map/psum | solution.py:67
  306.4 0.6 copy-start.2
  630.2 358.1 %copy-start.1 = (f32[8,3,64]{2,0,1:T(8,128)}, f32[8,3,64]{2,0,1:T(8,128)S(1)}, u32[]{:S(2)}) copy-start(f32[8,3,64]{2,0,1:T(8,128)S(1)} %fusion.61) | copy-start | bytes 18436
  631.1 27.5 %all-to-all-start.1 = ((f32[32,1,1536]{2,1,0:T(1,128)}), f32[32,1,1536]{2,1,0:T(1,128)S(1)}, u32[]{:S(2)}, u32[]{:S(2)}) async-start(f32[32,1,1536]{2,1,0:T(1,128)} %reshape.151), calls=%async_computation.1 | async-start | bytes 393216 | tf_op jit(solution)/shard_map/all_to_all | solution.py:47
  639.8 242.8 %all-reduce.5.cloned.1.call-start = ((), (), s32[]{:S(2)}) async-start(), calls=%async_computation.3 | async-start | bytes 196608 | tf_op jit(solution)/shard_map/psum | solution.py:67
  781.0 0.6 copy-start.3
Sparse Core Ops, SparseCore 0:
  307.1 113.8 all-reduce.2
  781.8 100.7 all-reduce.4
